TPU v7x, 32 devices: a whole 2x2x4 slice. The times are simulated.
32 devices in a mesh: tm: 16 (over z, y, x), ffn: 2 (over core).
Axes of the slice: x: 2, y: 2, z: 4, core: 2. Of those that a mesh axis runs over, the one named last changes fastest.
Arguments:
- frames: bfloat16 [32768, 512], P('tm'), may hold values from -60 to 60
- upstream: bfloat16 [32768, 512], P('tm'), may hold values from -6 to 6
- recording: int32 [32768], replicated, may hold values from 0 to 3, never falling along the last dimension, each value on 1 to 16384 neighbouring positions
- first_gain: float32 [512], replicated, may hold values from 0.1 to 1.9
- query_weight: bfloat16 [512, 512], P(None, 'ffn'), may hold values from -0.5 to 0.5
- key_weight: bfloat16 [512, 512], P(None, 'ffn'), may hold values from -0.5 to 0.5
- value_weight: bfloat16 [512, 512], P(None, 'ffn'), may hold values from -0.25 to 0.25
- out_weight: bfloat16 [512, 512], P('ffn'), may hold values from -0.25 to 0.25
- second_gain: float32 [512], replicated, may hold values from 0.1 to 1.9
- inner_weight: bfloat16 [512, 2048], P(None, 'ffn'), may hold values from -0.25 to 0.25
- outer_weight: bfloat16 [2048, 512], P('ffn'), may hold values from -0.125 to 0.125
Outputs:
- grad_frames: float32 [32768, 512], P(('tm', 'ffn'))
- grad_query_weight: float32 [512, 512], P(None, 'ffn')
- grad_key_weight: float32 [512, 512], P(None, 'ffn')
- grad_value_weight: float32 [512, 512], P(None, 'ffn')
- grad_out_weight: float32 [512, 512], P('ffn')
- grad_inner_weight: float32 [512, 2048], P(None, 'ffn')
- grad_outer_weight: float32 [2048, 512], P('ffn')
Inputs may be any that keep to these rules, and one draw needn't show every extreme that they name: Ids never fall along time; each recording spans 1 to 16384 frames and one spans exactly that many.
All inputs are finite; a program needn't handle non-finite values.
Results may differ from a plain program's by a relative error of at most 0.025.
Values may be sent and summed in bfloat16 or wider, within the bound.
A program may use at most 128 MiB of HBM per device.

v0:
```python
import math
import jax
import jax.numpy as jnp
from jax import lax
from jax.sharding import PartitionSpec as P

HEAD_DIM = 64
HALF = 256
epsilon = 1e-05
masked_score = -1e30


def with_halo(cells, sides, width):
    for axis, dim in sides:
        count = lax.axis_size(axis)
        ends = count - 1
        head = lax.slice_in_dim(cells, 0, width, axis=dim)
        tail = lax.slice_in_dim(cells, cells.shape[dim] - width, cells.shape[dim], axis=dim)
        cells = jnp.concatenate(
            [
                lax.ppermute(tail, axis, [(i, (i + 1) % count) for i in range(ends)]),
                cells,
                lax.ppermute(head, axis, [((i + 1) % count, i) for i in range(ends)]),
            ],
            axis=dim,
        )
    return cells


def layer_norm(inputs):
    center = jnp.mean(inputs, axis=-1, keepdims=True)
    shifted = inputs - center
    inverse = lax.rsqrt(jnp.mean(shifted * shifted, axis=-1, keepdims=True) + epsilon)
    return (shifted * inverse, inverse)


def norm_back(grad_normed, scaled, inverse, gain):
    weighted = grad_normed * gain
    first_mean = jnp.mean(weighted, axis=-1, keepdims=True)
    second_mean = jnp.mean(weighted * scaled, axis=-1, keepdims=True)
    return inverse * (weighted - first_mean - scaled * second_mean)


def project(normed, weight):
    return jnp.dot(normed, weight, preferred_element_type=jnp.float32).astype(jnp.bfloat16)


def block_allowed(record_query, record_key):
    block_rows = record_query.shape[0]
    offsets = lax.broadcasted_iota(
        jnp.int32, (block_rows, 2 * block_rows), 1
    ) - lax.broadcasted_iota(jnp.int32, (block_rows, 2 * block_rows), 0)
    band = (offsets >= 0) & (offsets < block_rows)
    return band & (record_query[:, None] == record_key[None, :])


def masked_scores(query_block, key_block, allowed):
    scores = jnp.einsum(
        "qhd,khd->hqk", query_block, key_block, preferred_element_type=jnp.float32
    ) * HEAD_DIM ** (-0.5)
    return jnp.where(allowed[None], scores, masked_score)


def tile_scores(query_block, key_block, allowed):
    return masked_scores(query_block, key_block, allowed)


def softmax_rows(scores):
    peak = jnp.max(scores, axis=-1, keepdims=True)
    weights = jnp.exp(scores - peak)
    return weights / jnp.sum(weights, axis=-1, keepdims=True)


def score_grads(grad_block, value_tile):
    return jnp.einsum("qhd,khd->hqk", grad_block, value_tile, preferred_element_type=jnp.float32)


def query_grads(score_tile, key_tile):
    return jnp.einsum("hqk,khd->qhd", score_tile, key_tile, preferred_element_type=jnp.float32)


def key_grads(score_tile, query_block):
    return jnp.einsum("hqk,qhd->khd", score_tile, query_block, preferred_element_type=jnp.float32)


def block_context(query_block, key_block, value_block, allowed):
    probability = softmax_rows(tile_scores(query_block, key_block, allowed))
    context = jnp.einsum(
        "hqk,khd->qhd",
        probability.astype(jnp.bfloat16),
        value_block,
        preferred_element_type=jnp.float32,
    )
    return context.astype(jnp.bfloat16)


def block_backward(query_block, key_block, value_block, grad_block, allowed):
    probability = softmax_rows(tile_scores(query_block, key_block, allowed))
    probability_low = probability.astype(jnp.bfloat16)
    grad_prob = score_grads(grad_block, value_block)
    inner_sum = jnp.sum(grad_prob * probability, axis=-1, keepdims=True)
    grad_scores = (probability * (grad_prob - inner_sum) * HEAD_DIM ** (-0.5)).astype(jnp.bfloat16)
    grad_query = query_grads(grad_scores, key_block)
    grad_key = key_grads(grad_scores, query_block)
    grad_value = key_grads(probability_low, grad_block)
    return (grad_query, grad_key, grad_value)


def local(
    frames,
    upstream,
    recording,
    first_gain,
    query_weight,
    key_weight,
    value_weight,
    out_weight,
    second_gain,
    inner_weight,
    outer_weight,
):
    slab_rows = frames.shape[0]
    block_rows = 2 * HALF
    head_cols = query_weight.shape[1]
    local_heads = head_cols // HEAD_DIM
    share_rows = slab_rows // lax.axis_size("ffn")
    share_start = lax.axis_index("ffn") * share_rows
    record_pad = jnp.pad(recording, (HALF, HALF), constant_values=-1)
    record_ext = lax.dynamic_slice_in_dim(
        record_pad, lax.axis_index("tm") * slab_rows, slab_rows + 2 * HALF
    )
    frames_wide = frames.astype(jnp.float32)
    upstream_wide = upstream.astype(jnp.float32)
    scaled_first, inverse_first = layer_norm(frames_wide)
    normed_first = (scaled_first * first_gain).astype(jnp.bfloat16)
    queries = project(normed_first, query_weight)
    key_rows = project(normed_first, key_weight)
    value_rows = project(normed_first, value_weight)
    key_value = jnp.concatenate([key_rows, value_rows], axis=1)
    key_value_ext = with_halo(key_value, (("tm", 0),), HALF)
    blocks = slab_rows // block_rows
    pieces = []
    contexts = []
    for block_index in range(blocks):
        first_row = block_index * block_rows
        query_block = queries[first_row : first_row + block_rows].reshape(
            block_rows, local_heads, HEAD_DIM
        )
        ext_block = key_value_ext[first_row : first_row + 2 * block_rows]
        key_block = ext_block[:, :head_cols].reshape(2 * block_rows, local_heads, HEAD_DIM)
        value_block = ext_block[:, head_cols:].reshape(2 * block_rows, local_heads, HEAD_DIM)
        allowed = block_allowed(
            record_ext[HALF + first_row : HALF + first_row + block_rows],
            record_ext[first_row : first_row + 2 * block_rows],
        )
        pieces.append((query_block, key_block, value_block, allowed))
        contexts.append(
            block_context(query_block, key_block, value_block, allowed).reshape(
                block_rows, head_cols
            )
        )
    context = jnp.concatenate(contexts, axis=0)
    partial_value = jnp.dot(context, out_weight, preferred_element_type=jnp.float32)
    middle = frames_wide + lax.psum(partial_value.astype(jnp.bfloat16), "ffn").astype(jnp.float32)
    scaled_second, inverse_second = layer_norm(middle)
    normed_second = (scaled_second * second_gain).astype(jnp.bfloat16)
    inner_pre = jnp.dot(normed_second, inner_weight, preferred_element_type=jnp.float32)
    activation = jax.nn.silu(inner_pre).astype(jnp.bfloat16)
    sigmoid_inner = jax.nn.sigmoid(inner_pre)
    grad_act = jnp.dot(upstream, outer_weight.T, preferred_element_type=jnp.float32) * 0.5
    grad_inner = (grad_act * sigmoid_inner * (1.0 + inner_pre * (1.0 - sigmoid_inner))).astype(
        jnp.bfloat16
    )
    grad_outer_terms = jnp.dot(activation.T, upstream, preferred_element_type=jnp.float32) * 0.5
    grad_inner_terms = jnp.dot(normed_second.T, grad_inner, preferred_element_type=jnp.float32)
    grad_second_part = jnp.dot(grad_inner, inner_weight.T, preferred_element_type=jnp.float32)
    grad_second = lax.psum(grad_second_part.astype(jnp.bfloat16), "ffn").astype(jnp.float32)
    grad_middle = upstream_wide + norm_back(grad_second, scaled_second, inverse_second, second_gain)
    grad_middle_low = grad_middle.astype(jnp.bfloat16)
    grad_middle_share = lax.dynamic_slice_in_dim(grad_middle, share_start, share_rows, 0)
    grad_out_terms = jnp.dot(context.T, grad_middle_low, preferred_element_type=jnp.float32)
    grad_context = jnp.dot(
        grad_middle_low, out_weight.T, preferred_element_type=jnp.float32
    ).astype(jnp.bfloat16)
    grad_pairs_ext = jnp.zeros((slab_rows + 2 * HALF, 2 * head_cols), jnp.float32)
    query_parts = []
    for block_index, (query_block, key_block, value_block, allowed) in enumerate(pieces):
        first_row = block_index * block_rows
        grad_block = grad_context[first_row : first_row + block_rows].reshape(
            block_rows, local_heads, HEAD_DIM
        )
        grad_query, grad_key, grad_value = block_backward(
            query_block, key_block, value_block, grad_block, allowed
        )
        query_parts.append(grad_query.reshape(block_rows, head_cols))
        grad_pair = jnp.concatenate(
            [
                grad_key.reshape(2 * block_rows, head_cols),
                grad_value.reshape(2 * block_rows, head_cols),
            ],
            axis=1,
        )
        grad_pairs_ext = grad_pairs_ext.at[first_row : first_row + 2 * block_rows].add(grad_pair)
    outer_rims = jnp.concatenate(
        [grad_pairs_ext[:HALF], grad_pairs_ext[slab_rows + HALF :]], axis=0
    )
    received = with_halo(outer_rims.astype(jnp.bfloat16), (("tm", 0),), HALF).astype(
        outer_rims.dtype
    )
    from_lower = received[:HALF]
    from_upper = received[3 * HALF :]
    grad_pairs = grad_pairs_ext[HALF : HALF + slab_rows]
    grad_pairs = (
        grad_pairs
        + jnp.pad(from_lower, ((0, slab_rows - HALF), (0, 0)))
        + jnp.pad(from_upper, ((slab_rows - HALF, 0), (0, 0)))
    )
    grad_query_low = jnp.concatenate(query_parts, axis=0).astype(jnp.bfloat16)
    grad_key_low = grad_pairs[:, :head_cols].astype(jnp.bfloat16)
    grad_value_low = grad_pairs[:, head_cols:].astype(jnp.bfloat16)
    grad_query_terms = jnp.dot(normed_first.T, grad_query_low, preferred_element_type=jnp.float32)
    grad_key_terms = jnp.dot(normed_first.T, grad_key_low, preferred_element_type=jnp.float32)
    grad_value_terms = jnp.dot(normed_first.T, grad_value_low, preferred_element_type=jnp.float32)
    grad_first_part = jnp.dot(grad_query_low, query_weight.T, preferred_element_type=jnp.float32)
    grad_first_part = grad_first_part + jnp.dot(
        grad_key_low, key_weight.T, preferred_element_type=jnp.float32
    )
    grad_first_part = grad_first_part + jnp.dot(
        grad_value_low, value_weight.T, preferred_element_type=jnp.float32
    )
    grad_first_share = lax.psum_scatter(
        grad_first_part.astype(jnp.bfloat16), "ffn", scatter_dimension=0, tiled=True
    ).astype(jnp.float32)
    scaled_share = lax.dynamic_slice_in_dim(scaled_first, share_start, share_rows, 0)
    inverse_share = lax.dynamic_slice_in_dim(inverse_first, share_start, share_rows, 0)
    grad_frames = grad_middle_share + norm_back(
        grad_first_share, scaled_share, inverse_share, first_gain
    )
    weight_scale = 1.0 / math.sqrt(recording.shape[0])
    totals = (
        lax.psum(grad_query_terms.astype(jnp.bfloat16), "tm").astype(jnp.float32),
        lax.psum(grad_key_terms.astype(jnp.bfloat16), "tm").astype(jnp.float32),
        lax.psum(grad_value_terms.astype(jnp.bfloat16), "tm").astype(jnp.float32),
        lax.psum(grad_out_terms.astype(jnp.bfloat16), "tm").astype(jnp.float32),
        lax.psum(grad_inner_terms.astype(jnp.bfloat16), "tm").astype(jnp.float32),
        lax.psum(grad_outer_terms.astype(jnp.bfloat16), "tm").astype(jnp.float32),
    )
    return (grad_frames,) + tuple((total * weight_scale for total in totals))


def solution(mesh):
    in_specs = (
        P("tm", None),
        P("tm", None),
        P(),
        P(),
        P(None, "ffn"),
        P(None, "ffn"),
        P(None, "ffn"),
        P("ffn", None),
        P(),
        P(None, "ffn"),
        P("ffn", None),
    )
    out_specs = (
        P(("tm", "ffn"), None),
        P(None, "ffn"),
        P(None, "ffn"),
        P(None, "ffn"),
        P("ffn", None),
        P(None, "ffn"),
        P("ffn", None),
    )
    return jax.shard_map(local, mesh=mesh, in_specs=in_specs, out_specs=out_specs, check_vma=False)
```

profile of v0, /device:TPU:0, one launch (start us, length us, event | category | flops | bytes accessed | tf_op | source)
XLA Modules:
  0.0 560.0 jit_solution(10052441508470068500)
XLA Ops:
  7.3 2.1 convert_reduce_fusion
  9.4 2.5 fusion.26
  11.9 2.4 fusion.24
  16.8 5.6 collective-permute-start
  27.4 2.3 convolution_convert_fusion.3
  30.6 2.5 collective-permute-done
  35.1 3.2 pad_maximum_fusion.5
  38.3 7.5 %fusion.168 = (f32[4,512]{1,0:T(4,128)S(1)}, f32[4,512,1024]{2,1,0:T(8,128)}) fusion(pred[512,1024]{1,0:T(8,128)(4,1)} %get-tuple-element.110, bf16[512,4,64]{0,2,1:T(8,128)(2,1)} %bitcast.159, bf16[1024,4,64]{0,2,1:T(8,128)(2,1)} %bitcast.151), kind=kOutput, calls=%fused_computation.222 | convolution fusion | flops 276825088 | bytes 9707520 | tf_op jit(solution)/shard_map/sub | solution.py:70
  45.7 5.7 %fusion.92 = bf16[4,64,512]{2,1,0:T(8,128)(2,1)} fusion(bf16[1024,4,64]{0,2,1:T(8,128)(2,1)} %bitcast.127, f32[4,512,1024]{2,1,0:T(8,128)} %get-tuple-element.106, f32[4,512]{1,0:T(4,128)S(1)} %get-tuple-element.105), kind=kOutput, calls=%fused_computation.125 | convolution fusion | flops 272760832 | bytes 9183232 | tf_op jit(solution)/shard_map/hqk,khd->qhd/dot_general | solution.py:88
  51.5 7.4 %fusion.165 = (f32[4,512]{1,0:T(4,128)S(1)}, f32[4,512,1024]{2,1,0:T(8,128)}) fusion(pred[512,1024]{1,0:T(8,128)(4,1)} %get-tuple-element.107, bf16[512,4,64]{0,2,1:T(8,128)(2,1)S(1)} %bitcast.157, bf16[1024,4,64]{0,2,1:T(8,128)(2,1)} %bitcast.149), kind=kOutput, calls=%fused_computation.219 | convolution fusion | flops 276825088 | bytes 9707520 | tf_op jit(solution)/shard_map/sub | solution.py:70
  58.9 5.8 %fusion.101 = bf16[4,64,512]{2,1,0:T(8,128)(2,1)} fusion(bf16[1024,4,64]{0,2,1:T(8,128)(2,1)} %bitcast.125, f32[4,512,1024]{2,1,0:T(8,128)} %get-tuple-element.100, f32[4,512]{1,0:T(4,128)S(1)} %get-tuple-element.99), kind=kOutput, calls=%fused_computation.128 | convolution fusion | flops 272760832 | bytes 9183232 | tf_op jit(solution)/shard_map/hqk,khd->qhd/dot_general | solution.py:88
  64.7 7.7 %fusion.166 = (f32[4,512]{1,0:T(4,128)S(1)}, f32[4,512,1024]{2,1,0:T(8,128)}) fusion(pred[512,1024]{1,0:T(8,128)(4,1)} %get-tuple-element.108, bf16[512,4,64]{0,2,1:T(8,128)(2,1)S(1)} %bitcast.161, bf16[1024,4,64]{0,2,1:T(8,128)(2,1)} %bitcast.153), kind=kOutput, calls=%fused_computation.220 | convolution fusion | flops 276825088 | bytes 9707520 | tf_op jit(solution)/shard_map/sub | solution.py:70
  72.4 5.8 %fusion.98 = bf16[4,64,512]{2,1,0:T(8,128)(2,1)} fusion(bf16[1024,4,64]{0,2,1:T(8,128)(2,1)} %bitcast.129, f32[4,512,1024]{2,1,0:T(8,128)} %get-tuple-element.102, f32[4,512]{1,0:T(4,128)S(1)} %get-tuple-element.101), kind=kOutput, calls=%fused_computation.127 | convolution fusion | flops 272760832 | bytes 9183232 | tf_op jit(solution)/shard_map/hqk,khd->qhd/dot_general | solution.py:88
  78.1 7.4 %fusion.167 = (f32[4,512]{1,0:T(4,128)S(1)}, f32[4,512,1024]{2,1,0:T(8,128)}) fusion(pred[512,1024]{1,0:T(8,128)(4,1)} %get-tuple-element.109, bf16[512,4,64]{0,2,1:T(8,128)(2,1)S(1)} %bitcast.163, bf16[1024,4,64]{0,2,1:T(8,128)(2,1)} %bitcast.155), kind=kOutput, calls=%fused_computation.221 | convolution fusion | flops 276825088 | bytes 9707520 | tf_op jit(solution)/shard_map/sub | solution.py:70
  85.6 5.1 fusion.95
  93.9 21.3 %all-reduce.9.cloned.1.call-done = bf16[2048,512]{1,0:T(8,128)(2,1)} async-done(((bf16[2048,512]{1,0:T(8,128)(2,1)}), bf16[2048,512]{1,0:T(8,128)(2,1)}) %all-reduce.9.cloned.1.call-update) | async-done | bytes 2097168 | tf_op jit(solution)/shard_map/psum | solution.py:164
  115.2 2.4 fusion.68
  118.6 2.8 fusion.162
  121.4 5.3 multiply_convert_fusion.5
  128.7 3.8 convolution_convert_fusion
  132.5 6.5 %convolution_convert_fusion.6 = bf16[512,1024]{1,0:T(8,128)(2,1)} fusion(bf16[2048,1024]{1,0:T(8,128)(2,1)} %copy-done.67, bf16[2048,512]{1,0:T(8,128)(2,1)} %all-reduce.9.cloned.1.call-done, bf16[2048,512]{1,0:T(8,128)(2,1)S(1)} %copy-done.2, f32[512]{0:T(512)S(1)} %copy-done.55, f32[2048]{0:T(1024)S(1)} %add_rsqrt_fusion, ...), kind=kOutput, calls=%fused_computation.124 | convolution fusion | flops 2155347968 | bytes 9455616 | tf_op jit(solution)/shard_map/dot_general | solution.py:175
  139.0 3.4 multiply_convert_fusion.9
  142.4 12.7 %all-reduce.11.cloned.1.call-done = bf16[2048,512]{1,0:T(8,128)(2,1)} async-done(((bf16[2048,512]{1,0:T(8,128)(2,1)}), bf16[2048,512]{1,0:T(8,128)(2,1)}) %all-reduce.11.cloned.1.call-update) | async-done | bytes 2097168 | tf_op jit(solution)/shard_map/psum | solution.py:177
  155.1 4.0 fusion.29
  159.2 2.3 multiply_add_fusion
  167.4 4.5 fusion.170
  171.9 22.1 %fusion.110 = bf16[4,64,512]{2,1,0:T(8,128)(2,1)} fusion(bf16[1024,4,64]{0,2,1:T(8,128)(2,1)S(1)} %bitcast.156, f32[4,512,1024]{2,1,0:T(8,128)} %fusion.170, f32[4,512,1024]{2,1,0:T(8,128)} %get-tuple-element.104, f32[4,512]{1,0:T(4,128)S(1)} %get-tuple-element.103), kind=kOutput, calls=%fused_computation.131 | convolution fusion | flops 283249664 | bytes 17571840 | tf_op jit(solution)/shard_map/hqk,khd->qhd/dot_general | solution.py:79
  194.1 18.3 %fusion.50 = f32[4,64,1024]{2,1,0:T(8,128)} fusion(bf16[512,4,64]{0,2,1:T(8,128)(2,1)S(1)} %bitcast.164, f32[4,512,1024]{2,1,0:T(8,128)} %fusion.170, f32[4,512,1024]{2,1,0:T(8,128)} %get-tuple-element.104, f32[4,512]{1,0:T(4,128)S(1)} %get-tuple-element.103), kind=kOutput, calls=%fused_computation.73 | convolution fusion | flops 283118592 | bytes 18096128 | tf_op jit(solution)/shard_map/hqk,qhd->khd/dot_general | solution.py:83
  212.4 5.3 fusion.77
  217.7 4.5 fusion.171
  222.2 21.9 %fusion.107 = bf16[4,64,512]{2,1,0:T(8,128)(2,1)} fusion(bf16[1024,4,64]{0,2,1:T(8,128)(2,1)S(1)} %bitcast.154, f32[4,512,1024]{2,1,0:T(8,128)} %fusion.171, f32[4,512,1024]{2,1,0:T(8,128)} %get-tuple-element.102, f32[4,512]{1,0:T(4,128)S(1)} %get-tuple-element.101), kind=kOutput, calls=%fused_computation.130 | convolution fusion | flops 283249664 | bytes 17571840 | tf_op jit(solution)/shard_map/hqk,khd->qhd/dot_general | solution.py:79
  244.2 18.5 %fusion.56 = f32[4,64,1024]{2,1,0:T(8,128)} fusion(bf16[512,4,64]{0,2,1:T(8,128)(2,1)S(1)} %bitcast.162, f32[4,512,1024]{2,1,0:T(8,128)} %fusion.171, f32[4,512,1024]{2,1,0:T(8,128)} %get-tuple-element.102, f32[4,512]{1,0:T(4,128)S(1)} %get-tuple-element.101), kind=kOutput, calls=%fused_computation.75 | convolution fusion | flops 283118592 | bytes 18096128 | tf_op jit(solution)/shard_map/hqk,qhd->khd/dot_general | solution.py:83
  262.7 4.4 fusion.85
  267.1 4.6 fusion.169
  271.7 21.9 %fusion.113 = bf16[4,64,512]{2,1,0:T(8,128)(2,1)} fusion(bf16[1024,4,64]{0,2,1:T(8,128)(2,1)S(1)} %bitcast.152, f32[4,512,1024]{2,1,0:T(8,128)} %fusion.169, f32[4,512,1024]{2,1,0:T(8,128)} %get-tuple-element.106, f32[4,512]{1,0:T(4,128)S(1)} %copy-done.71), kind=kOutput, calls=%fused_computation.132 | convolution fusion | flops 283249664 | bytes 17571840 | tf_op jit(solution)/shard_map/hqk,khd->qhd/dot_general | solution.py:79
  293.6 18.3 %fusion.44 = f32[4,64,1024]{2,1,0:T(8,128)} fusion(bf16[512,4,64]{0,2,1:T(8,128)(2,1)S(1)} %bitcast.160, f32[4,512,1024]{2,1,0:T(8,128)} %fusion.169, f32[4,512,1024]{2,1,0:T(8,128)} %get-tuple-element.106, f32[4,512]{1,0:T(4,128)S(1)} %copy-done.71), kind=kOutput, calls=%fused_computation.71 | convolution fusion | flops 283118592 | bytes 18096128 | tf_op jit(solution)/shard_map/hqk,qhd->khd/dot_general | solution.py:83
  311.9 4.4 fusion.73
  316.3 4.5 fusion.172
  320.8 21.9 %fusion.104 = bf16[4,64,512]{2,1,0:T(8,128)(2,1)} fusion(bf16[1024,4,64]{0,2,1:T(8,128)(2,1)S(1)} %bitcast.150, f32[4,512,1024]{2,1,0:T(8,128)} %fusion.172, f32[4,512,1024]{2,1,0:T(8,128)} %get-tuple-element.100, f32[4,512]{1,0:T(4,128)S(1)} %copy-done.69), kind=kOutput, calls=%fused_computation.129 | convolution fusion | flops 283249664 | bytes 17571840 | tf_op jit(solution)/shard_map/hqk,khd->qhd/dot_general | solution.py:79
  342.7 18.6 %fusion.62 = f32[4,64,1024]{2,1,0:T(8,128)} fusion(bf16[512,4,64]{0,2,1:T(8,128)(2,1)S(1)} %bitcast.158, f32[4,512,1024]{2,1,0:T(8,128)} %fusion.172, f32[4,512,1024]{2,1,0:T(8,128)} %get-tuple-element.100, f32[4,512]{1,0:T(4,128)S(1)} %copy-done.69), kind=kOutput, calls=%fused_computation.77 | convolution fusion | flops 283118592 | bytes 18096128 | tf_op jit(solution)/shard_map/hqk,qhd->khd/dot_general | solution.py:83
  367.0 4.6 collective-permute-start.2
  373.1 3.7 collective-permute-done.3
  376.8 6.0 %collective-permute-done.2 = bf16[256,512]{0,1:T(8,128)(2,1)S(1)} collective-permute-done((bf16[256,512]{0,1:T(8,128)(2,1)S(1)}, bf16[256,512]{0,1:T(8,128)(2,1)S(1)}, u32[]{:S(2)}, u32[]{:S(2)}) %collective-permute-start.2) | collective-permute-done | bytes 262176 | tf_op jit(solution)/shard_map/ppermute | solution.py:21
  389.0 2.1 add_convert_fusion
  391.2 143.1 %all-reduce.13.cloned.1.call-done = (bf16[512,256]{1,0:T(8,128)(2,1)}, bf16[512,256]{1,0:T(8,128)(2,1)}, bf16[512,256]{1,0:T(8,128)(2,1)}, bf16[256,512]{1,0:T(8...) async-done(((bf16[512,256]{1,0:T(8,128)(2,1)}, bf16[512,256]{1,0:T(8,128)(2,1)}, bf16[512,256]{1,0:T(8,128)(2,1)}, bf16[256,512]{1,0:T(8,128)(2,1)}, ...) | async-done | bytes 3145744 | tf_op jit(solution)/shard_map/psum | solution.py:241
  541.6 2.9 convert_multiply_fusion.2
  546.1 2.4 fusion.72
  548.6 4.4 multiply_add_fusion.1
  (203 shorter events, 44.7 us)
Async XLA Ops:
  7.2 111.4 %copy-start = (bf16[512,1024]{1,0:T(8,128)(2,1)S(1)}, bf16[512,1024]{1,0:T(8,128)(2,1)}, u32[]{:S(2)}) copy-start(bf16[512,1024]{1,0:T(8,128)(2,1)} %param.28) | copy-start | bytes 3145732
  7.2 4.7 copy-start.2
  7.2 4.7 copy-start.53
  7.2 108.0 %all-reduce.9.cloned.1.call-start = ((), (), s32[]{:S(2)}) async-start(), calls=%async_computation.1 | async-start | bytes 4194304 | tf_op jit(solution)/shard_map/psum | solution.py:164
  14.3 9.5 %copy-start.37 = (s32[32768]{0:T(1024)S(1)}, s32[32768]{0:T(1024)}, u32[]{:S(2)}) copy-start(s32[32768]{0:T(1024)} %param.21) | copy-start | bytes 393220
  15.1 12.3 %copy-start.31 = (bf16[512,256]{1,0:T(8,128)(2,1)S(1)}, bf16[512,256]{1,0:T(8,128)(2,1)}, u32[]{:S(2)}) copy-start(bf16[512,256]{1,0:T(8,128)(2,1)} %param.23) | copy-start | bytes 786436
  15.9 6.5 %copy-start.10 = (bf16[2048,256]{0,1:T(8,128)(2,1)}, bf16[2048,256]{0,1:T(8,128)(2,1)S(1)}, u32[]{:S(2)}) copy-start(bf16[2048,256]{0,1:T(8,128)(2,1)S(1)} %convolution_convert_fusion.5) | copy-start | bytes 3145732
  16.8 16.4 %collective-permute-start = (bf16[256,512]{0,1:T(8,128)(2,1)}, bf16[256,512]{0,1:T(8,128)(2,1)}, u32[]{:S(2)}, u32[]{:S(2)}) collective-permute-start(bf16[256,512]{0,1:T(8,128)(2,1)} %get-tuple-element.75), channel_id=1, source_target_pairs={{0,2},{2,4},{4,6},{6,8},{8,10},{10,12},{12,14},{14,16},{16,18},{18... | collective-permute-start | bytes 786440 | tf_op jit(solution)/shard_map/ppermute | solution.py:21
  22.4 12.7 %collective-permute-start.1 = (bf16[256,512]{0,1:T(8,128)(2,1)}, bf16[256,512]{0,1:T(8,128)(2,1)}, u32[]{:S(2)}, u32[]{:S(2)}) collective-permute-start(bf16[256,512]{0,1:T(8,128)(2,1)} %get-tuple-element.76), channel_id=1, source_target_pairs={{2,0},{4,2},{6,4},{8,6},{10,8},{12,10},{14,12},{16,14},{18,16},{20... | collective-permute-start | bytes 786440 | tf_op jit(solution)/shard_map/ppermute | solution.py:23
  23.8 11.2 %copy-start.9 = (bf16[2048,256]{0,1:T(8,128)(2,1)S(1)}, bf16[2048,256]{0,1:T(8,128)(2,1)}, u32[]{:S(2)}) copy-start(bf16[2048,256]{0,1:T(8,128)(2,1)} %copy-done.8) | copy-start | bytes 3145732
  23.8 11.2 %copy-start.11 = (bf16[2048,256]{0,1:T(8,128)(2,1)S(1)}, bf16[2048,256]{0,1:T(8,128)(2,1)}, u32[]{:S(2)}) copy-start(bf16[2048,256]{0,1:T(8,128)(2,1)} %copy-done.10) | copy-start | bytes 3145732
  30.6 20.9 %copy-start.38 = (bf16[512,256]{0,1:T(8,128)(2,1)}, bf16[512,256]{0,1:T(8,128)(2,1)S(1)}, u32[]{:S(2)}) copy-start(bf16[512,256]{0,1:T(8,128)(2,1)S(1)} %get-tuple-element.88) | copy-start | bytes 786436
  45.7 5.7 %copy-start.70 = (f32[4,512]{1,0:T(4,128)}, f32[4,512]{1,0:T(4,128)S(1)}, u32[]{:S(2)}) copy-start(f32[4,512]{1,0:T(4,128)S(1)} %get-tuple-element.105) | copy-start | bytes 24580
  58.9 5.8 %copy-start.68 = (f32[4,512]{1,0:T(4,128)}, f32[4,512]{1,0:T(4,128)S(1)}, u32[]{:S(2)}) copy-start(f32[4,512]{1,0:T(4,128)S(1)} %get-tuple-element.99) | copy-start | bytes 24580
  58.9 5.8 %copy-start.41 = (bf16[512,256]{0,1:T(8,128)(2,1)S(1)}, bf16[512,256]{0,1:T(8,128)(2,1)}, u32[]{:S(2)}) copy-start(bf16[512,256]{0,1:T(8,128)(2,1)} %get-tuple-element.89) | copy-start | bytes 786436
  72.4 5.8 %copy-start.43 = (bf16[512,256]{0,1:T(8,128)(2,1)S(1)}, bf16[512,256]{0,1:T(8,128)(2,1)}, u32[]{:S(2)}) copy-start(bf16[512,256]{0,1:T(8,128)(2,1)} %get-tuple-element.90) | copy-start | bytes 786436
  85.6 5.8 %copy-start.45 = (bf16[256,512]{1,0:T(8,128)(2,1)S(1)}, bf16[256,512]{1,0:T(8,128)(2,1)}, u32[]{:S(2)}) copy-start(bf16[256,512]{1,0:T(8,128)(2,1)} %param.26) | copy-start | bytes 786436
  85.6 5.8 %copy-start.57 = (bf16[4,64,512]{2,1,0:T(8,128)(2,1)S(1)}, bf16[4,64,512]{2,1,0:T(8,128)(2,1)}, u32[]{:S(2)}) copy-start(bf16[4,64,512]{2,1,0:T(8,128)(2,1)} %fusion.92) | copy-start | bytes 786436
  85.6 5.8 %copy-start.59 = (bf16[4,64,512]{2,1,0:T(8,128)(2,1)S(1)}, bf16[4,64,512]{2,1,0:T(8,128)(2,1)}, u32[]{:S(2)}) copy-start(bf16[4,64,512]{2,1,0:T(8,128)(2,1)} %fusion.101) | copy-start | bytes 786436
  85.6 5.8 %copy-start.61 = (bf16[4,64,512]{2,1,0:T(8,128)(2,1)S(1)}, bf16[4,64,512]{2,1,0:T(8,128)(2,1)}, u32[]{:S(2)}) copy-start(bf16[4,64,512]{2,1,0:T(8,128)(2,1)} %fusion.98) | copy-start | bytes 786436
  93.5 25.1 %copy-start.55 = (f32[512]{0:T(512)S(1)}, f32[512]{0:T(512)}, u32[]{:S(2)}) copy-start(f32[512]{0:T(512)} %param.27) | copy-start | bytes 6148
  93.5 61.6 %all-reduce.11.cloned.1.call-start = ((), (), s32[]{:S(2)}) async-start(), calls=%async_computation.2 | async-start | bytes 4194304 | tf_op jit(solution)/shard_map/psum | solution.py:177
  121.4 5.3 copy-start.65
  132.5 401.8 %all-reduce.13.cloned.1.call-start = ((), (), s32[]{:S(2)}) async-start(), calls=%async_computation.4 | async-start | bytes 6291456 | tf_op jit(solution)/shard_map/psum | solution.py:241
  132.5 6.5 %copy-start.18 = (bf16[2048,512]{1,0:T(8,128)(2,1)S(1)}, bf16[2048,512]{1,0:T(8,128)(2,1)}, u32[]{:S(2)}) copy-start(bf16[2048,512]{1,0:T(8,128)(2,1)} %param.20) | copy-start | bytes 6291460
  132.5 6.5 %copy-start.66 = (f32[2048,1024]{1,0:T(8,128)S(1)}, f32[2048,1024]{1,0:T(8,128)}, u32[]{:S(2)}) copy-start(f32[2048,1024]{1,0:T(8,128)} %copy-done.65) | copy-start | bytes 25165828
  159.2 4.8 slice-start
  171.9 22.1 %copy-start.44 = (bf16[512,256]{0,1:T(8,128)(2,1)S(1)}, bf16[512,256]{0,1:T(8,128)(2,1)}, u32[]{:S(2)}) copy-start(bf16[512,256]{0,1:T(8,128)(2,1)} %get-tuple-element.90) | copy-start | bytes 786436
  212.4 5.4 copy-start.15
  222.2 21.9 %copy-start.42 = (bf16[512,256]{0,1:T(8,128)(2,1)S(1)}, bf16[512,256]{0,1:T(8,128)(2,1)}, u32[]{:S(2)}) copy-start(bf16[512,256]{0,1:T(8,128)(2,1)} %get-tuple-element.89) | copy-start | bytes 786436
  244.2 18.5 %copy-start.71 = (f32[4,512]{1,0:T(4,128)S(1)}, f32[4,512]{1,0:T(4,128)}, u32[]{:S(2)}) copy-start(f32[4,512]{1,0:T(4,128)} %copy-done.70) | copy-start | bytes 24580
  267.1 4.6 copy-start.34
  271.7 21.9 %copy-start.40 = (bf16[512,256]{0,1:T(8,128)(2,1)S(1)}, bf16[512,256]{0,1:T(8,128)(2,1)}, u32[]{:S(2)}) copy-start(bf16[512,256]{0,1:T(8,128)(2,1)} %get-tuple-element.87) | copy-start | bytes 786436
  293.6 18.3 %copy-start.69 = (f32[4,512]{1,0:T(4,128)S(1)}, f32[4,512]{1,0:T(4,128)}, u32[]{:S(2)}) copy-start(f32[4,512]{1,0:T(4,128)} %copy-done.68) | copy-start | bytes 24580
  320.8 21.9 %copy-start.39 = (bf16[512,256]{0,1:T(8,128)(2,1)S(1)}, bf16[512,256]{0,1:T(8,128)(2,1)}, u32[]{:S(2)}) copy-start(bf16[512,256]{0,1:T(8,128)(2,1)} %copy-done.38) | copy-start | bytes 786436
  342.7 18.6 %copy-start.22 = (f32[4,64,1024]{2,1,0:T(8,128)S(1)}, f32[4,64,1024]{2,1,0:T(8,128)}, u32[]{:S(2)}) copy-start(f32[4,64,1024]{2,1,0:T(8,128)} %fusion.44) | copy-start | bytes 3145732
  364.7 6.9 %copy-start.4 = (bf16[2048,512]{1,0:T(8,128)(2,1)S(1)}, bf16[2048,512]{1,0:T(8,128)(2,1)}, u32[]{:S(2)}) copy-start(bf16[2048,512]{1,0:T(8,128)(2,1)} %copy-done.3) | copy-start | bytes 6291460
  364.7 6.9 %copy-start.46 = (bf16[4,64,512]{2,1,0:T(8,128)(2,1)S(1)}, bf16[4,64,512]{2,1,0:T(8,128)(2,1)}, u32[]{:S(2)}) copy-start(bf16[4,64,512]{2,1,0:T(8,128)(2,1)} %fusion.110) | copy-start | bytes 786436
  364.7 6.9 %copy-start.47 = (bf16[4,64,512]{2,1,0:T(8,128)(2,1)S(1)}, bf16[4,64,512]{2,1,0:T(8,128)(2,1)}, u32[]{:S(2)}) copy-start(bf16[4,64,512]{2,1,0:T(8,128)(2,1)} %fusion.107) | copy-start | bytes 786436
  364.7 6.9 %copy-start.49 = (bf16[4,64,512]{2,1,0:T(8,128)(2,1)S(1)}, bf16[4,64,512]{2,1,0:T(8,128)(2,1)}, u32[]{:S(2)}) copy-start(bf16[4,64,512]{2,1,0:T(8,128)(2,1)} %fusion.113) | copy-start | bytes 786436
  364.7 6.9 %copy-start.51 = (bf16[4,64,512]{2,1,0:T(8,128)(2,1)S(1)}, bf16[4,64,512]{2,1,0:T(8,128)(2,1)}, u32[]{:S(2)}) copy-start(bf16[4,64,512]{2,1,0:T(8,128)(2,1)} %fusion.104) | copy-start | bytes 786436
  365.7 11.1 %collective-permute-start.3 = (bf16[256,512]{0,1:T(8,128)(2,1)S(1)}, bf16[256,512]{0,1:T(8,128)(2,1)S(1)}, u32[]{:S(2)}, u32[]{:S(2)}) collective-permute-start(bf16[256,512]{0,1:T(8,128)(2,1)S(1)} %slice.275), channel_id=1, source_target_pairs={{2,0},{4,2},{6,4},{8,6},{10,8},{12,10},{14,12},{16,14},{18,16},{20... | collective-permute-start | bytes 786440 | tf_op jit(solution)/shard_map/ppermute | solution.py:23
  367.0 15.8 %collective-permute-start.2 = (bf16[256,512]{0,1:T(8,128)(2,1)S(1)}, bf16[256,512]{0,1:T(8,128)(2,1)S(1)}, u32[]{:S(2)}, u32[]{:S(2)}) collective-permute-start(bf16[256,512]{0,1:T(8,128)(2,1)S(1)} %slice.276), channel_id=1, source_target_pairs={{0,2},{2,4},{4,6},{6,8},{8,10},{10,12},{12,14},{14,16},{16,18},{18... | collective-permute-start | bytes 786440 | tf_op jit(solution)/shard_map/ppermute | solution.py:21
  386.3 159.8 %reduce-scatter.2.cloned.1.call-start = ((), (), s32[]{:S(2)}) async-start(), calls=%async_computation.3 | async-start | bytes 3145728 | tf_op jit(solution)/shard_map/reduce_scatter | solution.py:231
  534.3 10.2 %copy-start.20 = (bf16[1024,512]{1,0:T(8,128)(2,1)S(1)}, bf16[1024,512]{1,0:T(8,128)(2,1)}, u32[]{:S(2)}) copy-start(bf16[1024,512]{1,0:T(8,128)(2,1)} %get-tuple-element.64) | copy-start | bytes 3145732
  536.2 9.9 %copy-start.54 = (f32[512]{0:T(512)S(1)}, f32[512]{0:T(512)}, u32[]{:S(2)}) copy-start(f32[512]{0:T(512)} %param.22) | copy-start | bytes 6148
  541.6 7.0 %dynamic-slice-start = ((f32[2048]{0:T(1024)}, s32[]{:T(128)}), f32[1024]{0:T(1024)S(1)}, s32[]{:S(2)}) async-start(f32[2048]{0:T(1024)} %copy-done.52, s32[]{:T(128)} %select_n.30), calls=%async_computation.5 | async-start | bytes 8704 | tf_op jit(solution)/shard_map/dynamic-slice.31
  546.1 6.9 %copy-start.1 = (bf16[512,1024]{1,0:T(8,128)(2,1)S(1)}, bf16[512,1024]{1,0:T(8,128)(2,1)}, u32[]{:S(2)}) copy-start(bf16[512,1024]{1,0:T(8,128)(2,1)} %param.28) | copy-start | bytes 3145732
  (35 other events, 89.5 us)
Sparse Core Ops, SparseCore 0:
  93.6 21.5 all-reduce.8
  132.6 22.4 all-reduce.10
  386.4 147.8 all-reduce.12
  537.0 8.6 reduce-scatter.1
where the time goes:
time: 564 us; the launch traced here: 560 us
  matrix products  287 us (51%)
  waiting for transfers between devices  191 us (34%)
  other arithmetic  45.8 us (8%)
  between operations  15 us (3%)
  starting transfers between devices  13.4 us (2%)
  local copies, waits for them, and re-layouts  7.53 us (1%)
    psum x1, waiting for transfers between devices, local(): lax.psum(grad_query_terms.astype(jnp.bfloat16), 'tm').astype(jnp.float32)  143 us
    dot_general x8, matrix products, key_grads(): jnp.einsum('hqk,qhd->khd', score_tile, query_block, preferred_element_typ...  89.7 us
    dot_general x4, matrix products, query_grads(): jnp.einsum('hqk,khd->qhd', score_tile, key_tile, preferred_element_type=j...  87.9 us
    sub x4, matrix products, softmax_rows(): weights = jnp.exp(scores - peak)  30 us
    dot_general x4, matrix products, block_context(): jnp.einsum('hqk,khd->qhd', probability.astype(jnp.bfloat16), value_block,...  22.4 us
    psum x1, waiting for transfers between devices, local(): lax.psum(partial_value.astype(jnp.bfloat16), 'ffn').astype(jnp.float32)  21.3 us
    dot_general x4, matrix products, score_grads(): jnp.einsum('qhd,khd->hqk', grad_block, value_tile, preferred_element_type...  18.2 us
    psum x1, waiting for transfers between devices, local(): lax.psum(grad_second_part.astype(jnp.bfloat16), 'ffn').astype(jnp.float32)  12.7 us
  transfers between devices with their start and end apart: 8, of which 7 were waited for; matrix products, arithmetic and copies ran while one was open for 6% of the time, Pallas kernels for 0%

commit v1 on v0

--- a/solution.py
+++ b/solution.py
@@ -238,7 +238,9 @@
     )
     weight_scale = 1.0 / math.sqrt(recording.shape[0])
     totals = (
-        lax.psum(grad_query_terms.astype(jnp.bfloat16), "tm").astype(jnp.float32),
+        jnp.sum(lax.all_gather(grad_query_terms.astype(jnp.bfloat16), "tm"), axis=0).astype(
+            jnp.float32
+        ),
         lax.psum(grad_key_terms.astype(jnp.bfloat16), "tm").astype(jnp.float32),
         lax.psum(grad_value_terms.astype(jnp.bfloat16), "tm").astype(jnp.float32),
         lax.psum(grad_out_terms.astype(jnp.bfloat16), "tm").astype(jnp.float32),

time: 564 us -> 540 us (0.957)
  waiting for transfers between devices: 191 us -> 171 us
  matrix products: 287 us -> 281 us
    psum x1, waiting for transfers between devices: 143 us -> 47.9 us  [local(): lax.psum(grad_key_terms.astype(jnp.bfloat16), 'tm').astype(jnp.float32)]
    all_gather x0 -> x1, waiting for transfers between devices: none -> 73.2 us  [local(): lax.all_gather(grad_query_terms.astype(jnp.bfloat16), 'tm')]
    dot_general x8, matrix products: 89.7 us -> 83.5 us  [key_grads(): jnp.einsum('hqk,qhd->khd', score_tile, query_block, preferred_element_typ...]
  transfers between devices with their start and end apart: 8 -> 9, of which waited for: 7 -> 9; matrix products, arithmetic and copies ran while one was open for 6% -> 24% of each run, Pallas kernels for 0% -> 0%
where the time goes in v1:
time: 540 us; the launch traced here: 537 us
  matrix products  281 us (52%)
  waiting for transfers between devices  171 us (32%)
  other arithmetic  47.8 us (9%)
  between operations  15 us (3%)
  starting transfers between devices  14 us (3%)
  local copies, waits for them, and re-layouts  8.24 us (2%)
    dot_general x4, matrix products, query_grads(): jnp.einsum('hqk,khd->qhd', score_tile, key_tile, preferred_element_type=j...  87.9 us
    dot_general x8, matrix products, key_grads(): jnp.einsum('hqk,qhd->khd', score_tile, query_block, preferred_element_typ...  83.5 us
    all_gather x1, waiting for transfers between devices, local(): lax.all_gather(grad_query_terms.astype(jnp.bfloat16), 'tm')  73.2 us
    psum x1, waiting for transfers between devices, local(): lax.psum(grad_key_terms.astype(jnp.bfloat16), 'tm').astype(jnp.float32)  47.9 us
    sub x4, matrix products, softmax_rows(): weights = jnp.exp(scores - peak)  30 us
    dot_general x4, matrix products, block_context(): jnp.einsum('hqk,khd->qhd', probability.astype(jnp.bfloat16), value_block,...  22.3 us
    psum x1, waiting for transfers between devices, local(): lax.psum(partial_value.astype(jnp.bfloat16), 'ffn').astype(jnp.float32)  21.5 us
    dot_general x4, matrix products, score_grads(): jnp.einsum('qhd,khd->hqk', grad_block, value_tile, preferred_element_type...  18.1 us
  transfers between devices with their start and end apart: 9, of which 9 were waited for; matrix products, arithmetic and copies ran while one was open for 24% of the time, Pallas kernels for 0%

profile of v1, /device:TPU:0, one launch (start us, length us, event | category | flops | bytes accessed | tf_op | source)
XLA Modules:
  0.0 536.6 jit_solution(14578448574849368625)
XLA Ops:
  7.3 2.1 convert_reduce_fusion
  9.4 2.5 fusion.26
  11.9 2.4 fusion.24
  16.8 5.6 %collective-permute-start = (bf16[256,512]{0,1:T(8,128)(2,1)}, bf16[256,512]{0,1:T(8,128)(2,1)}, u32[]{:S(2)}, u32[]{:S(2)}) collective-permute-start(bf16[256,512]{0,1:T(8,128)(2,1)} %get-tuple-element.74), channel_id=1, source_target_pairs={{0,2},{2,4},{4,6},{6,8},{8,10},{10,12},{12,14},{14,16},{16,18},{18... | collective-permute-start | bytes 786440 | tf_op jit(solution)/shard_map/ppermute | solution.py:21
  27.8 2.3 convolution_convert_fusion.3
  31.1 2.1 collective-permute-done
  35.1 3.2 pad_maximum_fusion.5
  38.3 7.5 %fusion.168 = (f32[4,512]{1,0:T(4,128)S(1)}, f32[4,512,1024]{2,1,0:T(8,128)}) fusion(pred[512,1024]{1,0:T(8,128)(4,1)} %get-tuple-element.109, bf16[512,4,64]{0,2,1:T(8,128)(2,1)} %bitcast.161, bf16[1024,4,64]{0,2,1:T(8,128)(2,1)} %bitcast.153), kind=kOutput, calls=%fused_computation.222 | convolution fusion | flops 276825088 | bytes 9707520 | tf_op jit(solution)/shard_map/sub | solution.py:70
  45.8 5.7 %fusion.92 = bf16[4,64,512]{2,1,0:T(8,128)(2,1)} fusion(bf16[1024,4,64]{0,2,1:T(8,128)(2,1)} %bitcast.129, f32[4,512,1024]{2,1,0:T(8,128)} %get-tuple-element.105, f32[4,512]{1,0:T(4,128)S(1)} %get-tuple-element.104), kind=kOutput, calls=%fused_computation.125 | convolution fusion | flops 272760832 | bytes 9183232 | tf_op jit(solution)/shard_map/hqk,khd->qhd/dot_general | solution.py:88
  51.6 7.4 %fusion.165 = (f32[4,512]{1,0:T(4,128)S(1)}, f32[4,512,1024]{2,1,0:T(8,128)}) fusion(pred[512,1024]{1,0:T(8,128)(4,1)} %get-tuple-element.106, bf16[512,4,64]{0,2,1:T(8,128)(2,1)S(1)} %bitcast.159, bf16[1024,4,64]{0,2,1:T(8,128)(2,1)} %bitcast.151), kind=kOutput, calls=%fused_computation.219 | convolution fusion | flops 276825088 | bytes 9707520 | tf_op jit(solution)/shard_map/sub | solution.py:70
  59.0 5.8 %fusion.101 = bf16[4,64,512]{2,1,0:T(8,128)(2,1)} fusion(bf16[1024,4,64]{0,2,1:T(8,128)(2,1)} %bitcast.127, f32[4,512,1024]{2,1,0:T(8,128)} %get-tuple-element.99, f32[4,512]{1,0:T(4,128)S(1)} %get-tuple-element.98), kind=kOutput, calls=%fused_computation.128 | convolution fusion | flops 272760832 | bytes 9183232 | tf_op jit(solution)/shard_map/hqk,khd->qhd/dot_general | solution.py:88
  64.7 7.6 %fusion.166 = (f32[4,512]{1,0:T(4,128)S(1)}, f32[4,512,1024]{2,1,0:T(8,128)}) fusion(pred[512,1024]{1,0:T(8,128)(4,1)} %get-tuple-element.107, bf16[512,4,64]{0,2,1:T(8,128)(2,1)S(1)} %bitcast.163, bf16[1024,4,64]{0,2,1:T(8,128)(2,1)} %bitcast.155), kind=kOutput, calls=%fused_computation.220 | convolution fusion | flops 276825088 | bytes 9707520 | tf_op jit(solution)/shard_map/sub | solution.py:70
  72.3 5.7 %fusion.98 = bf16[4,64,512]{2,1,0:T(8,128)(2,1)} fusion(bf16[1024,4,64]{0,2,1:T(8,128)(2,1)} %bitcast.131, f32[4,512,1024]{2,1,0:T(8,128)} %get-tuple-element.101, f32[4,512]{1,0:T(4,128)S(1)} %get-tuple-element.100), kind=kOutput, calls=%fused_computation.127 | convolution fusion | flops 272760832 | bytes 9183232 | tf_op jit(solution)/shard_map/hqk,khd->qhd/dot_general | solution.py:88
  78.1 7.5 %fusion.167 = (f32[4,512]{1,0:T(4,128)S(1)}, f32[4,512,1024]{2,1,0:T(8,128)}) fusion(pred[512,1024]{1,0:T(8,128)(4,1)} %get-tuple-element.108, bf16[512,4,64]{0,2,1:T(8,128)(2,1)} %bitcast.165, bf16[1024,4,64]{0,2,1:T(8,128)(2,1)} %bitcast.157), kind=kOutput, calls=%fused_computation.221 | convolution fusion | flops 276825088 | bytes 9707520 | tf_op jit(solution)/shard_map/sub | solution.py:70
  85.6 5.1 fusion.95
  91.4 2.1 convolution_convert_fusion.1
  93.7 21.5 %all-reduce.9.cloned.1.call-done = bf16[2048,512]{1,0:T(8,128)(2,1)} async-done(((bf16[2048,512]{1,0:T(8,128)(2,1)}), bf16[2048,512]{1,0:T(8,128)(2,1)}) %all-reduce.9.cloned.1.call-update) | async-done | bytes 2097168 | tf_op jit(solution)/shard_map/psum | solution.py:164
  115.2 2.4 fusion.68
  118.6 2.8 fusion.162
  121.4 5.3 multiply_convert_fusion.5
  128.7 3.8 convolution_convert_fusion
  132.5 6.5 %convolution_convert_fusion.6 = bf16[512,1024]{1,0:T(8,128)(2,1)} fusion(bf16[2048,1024]{1,0:T(8,128)(2,1)} %copy-done.64, bf16[2048,512]{1,0:T(8,128)(2,1)} %all-reduce.9.cloned.1.call-done, bf16[2048,512]{1,0:T(8,128)(2,1)S(1)} %copy-done.2, f32[512]{0:T(512)S(1)} %copy-done.52, f32[2048]{0:T(1024)S(1)} %add_rsqrt_fusion, ...), kind=kOutput, calls=%fused_computation.124 | convolution fusion | flops 2155347968 | bytes 9455616 | tf_op jit(solution)/shard_map/dot_general | solution.py:175
  139.0 3.4 multiply_convert_fusion.9
  142.4 12.7 %all-reduce.11.cloned.1.call-done = bf16[2048,512]{1,0:T(8,128)(2,1)} async-done(((bf16[2048,512]{1,0:T(8,128)(2,1)}), bf16[2048,512]{1,0:T(8,128)(2,1)}) %all-reduce.11.cloned.1.call-update) | async-done | bytes 2097168 | tf_op jit(solution)/shard_map/psum | solution.py:177
  155.1 4.1 fusion.29
  159.2 2.3 multiply_add_fusion
  165.5 4.5 fusion.170
  172.0 4.5 fusion.171
  177.8 4.5 fusion.169
  183.5 4.5 fusion.172
  188.1 18.3 %fusion.50 = f32[4,64,1024]{2,1,0:T(8,128)} fusion(bf16[512,4,64]{0,2,1:T(8,128)(2,1)S(1)} %bitcast.166, f32[4,512,1024]{2,1,0:T(8,128)} %fusion.170, f32[4,512,1024]{2,1,0:T(8,128)} %get-tuple-element.103, f32[4,512]{1,0:T(4,128)S(1)} %get-tuple-element.102), kind=kOutput, calls=%fused_computation.73 | convolution fusion | flops 283118592 | bytes 18096128 | tf_op jit(solution)/shard_map/hqk,qhd->khd/dot_general | solution.py:83
  206.3 18.5 %fusion.56 = f32[4,64,1024]{2,1,0:T(8,128)} fusion(bf16[512,4,64]{0,2,1:T(8,128)(2,1)S(1)} %bitcast.164, f32[4,512,1024]{2,1,0:T(8,128)} %fusion.171, f32[4,512,1024]{2,1,0:T(8,128)} %get-tuple-element.101, f32[4,512]{1,0:T(4,128)S(1)} %get-tuple-element.100), kind=kOutput, calls=%fused_computation.75 | convolution fusion | flops 283118592 | bytes 18096128 | tf_op jit(solution)/shard_map/hqk,qhd->khd/dot_general | solution.py:83
  224.8 22.2 %fusion.44 = f32[4,64,1024]{2,1,0:T(8,128)S(1)} fusion(bf16[512,4,64]{0,2,1:T(8,128)(2,1)} %bitcast.162, f32[4,512,1024]{2,1,0:T(8,128)} %fusion.169, f32[4,512,1024]{2,1,0:T(8,128)} %get-tuple-element.105, f32[4,512]{1,0:T(4,128)S(1)} %get-tuple-element.104), kind=kOutput, calls=%fused_computation.71 | convolution fusion | flops 283118592 | bytes 18096128 | tf_op jit(solution)/shard_map/hqk,qhd->khd/dot_general | solution.py:83
  247.0 18.3 %fusion.62 = f32[4,64,1024]{2,1,0:T(8,128)} fusion(bf16[512,4,64]{0,2,1:T(8,128)(2,1)S(1)} %bitcast.160, f32[4,512,1024]{2,1,0:T(8,128)} %fusion.172, f32[4,512,1024]{2,1,0:T(8,128)} %get-tuple-element.99, f32[4,512]{1,0:T(4,128)S(1)} %get-tuple-element.98), kind=kOutput, calls=%fused_computation.77 | convolution fusion | flops 283118592 | bytes 18096128 | tf_op jit(solution)/shard_map/hqk,qhd->khd/dot_general | solution.py:83
  271.2 4.6 collective-permute-start.2
  277.2 3.7 collective-permute-done.3
  280.9 6.0 %collective-permute-done.2 = bf16[256,512]{0,1:T(8,128)(2,1)S(1)} collective-permute-done((bf16[256,512]{0,1:T(8,128)(2,1)S(1)}, bf16[256,512]{0,1:T(8,128)(2,1)S(1)}, u32[]{:S(2)}, u32[]{:S(2)}) %collective-permute-start.2) | collective-permute-done | bytes 262176 | tf_op jit(solution)/shard_map/ppermute | solution.py:21
  291.6 21.7 %fusion.110 = bf16[4,64,512]{2,1,0:T(8,128)(2,1)S(1)} fusion(bf16[1024,4,64]{0,2,1:T(8,128)(2,1)S(1)} %bitcast.158, f32[4,512,1024]{2,1,0:T(8,128)} %fusion.170, f32[4,512,1024]{2,1,0:T(8,128)} %get-tuple-element.103, f32[4,512]{1,0:T(4,128)S(1)} %get-tuple-element.102), kind=kOutput, calls=%fused_computation.131 | convolution fusion | flops 283249664 | bytes 17571840 | tf_op jit(solution)/shard_map/hqk,khd->qhd/dot_general | solution.py:79
  313.4 22.1 %fusion.107 = bf16[4,64,512]{2,1,0:T(8,128)(2,1)} fusion(bf16[1024,4,64]{0,2,1:T(8,128)(2,1)S(1)} %bitcast.156, f32[4,512,1024]{2,1,0:T(8,128)} %fusion.171, f32[4,512,1024]{2,1,0:T(8,128)} %get-tuple-element.101, f32[4,512]{1,0:T(4,128)S(1)} %get-tuple-element.100), kind=kOutput, calls=%fused_computation.130 | convolution fusion | flops 283249664 | bytes 17571840 | tf_op jit(solution)/shard_map/hqk,khd->qhd/dot_general | solution.py:79
  335.5 22.1 %fusion.113 = bf16[4,64,512]{2,1,0:T(8,128)(2,1)} fusion(bf16[1024,4,64]{0,2,1:T(8,128)(2,1)S(1)} %bitcast.154, f32[4,512,1024]{2,1,0:T(8,128)} %fusion.169, f32[4,512,1024]{2,1,0:T(8,128)} %get-tuple-element.105, f32[4,512]{1,0:T(4,128)S(1)} %get-tuple-element.104), kind=kOutput, calls=%fused_computation.132 | convolution fusion | flops 283249664 | bytes 17571840 | tf_op jit(solution)/shard_map/hqk,khd->qhd/dot_general | solution.py:79
  357.6 22.0 %fusion.104 = bf16[4,64,512]{2,1,0:T(8,128)(2,1)} fusion(bf16[1024,4,64]{0,2,1:T(8,128)(2,1)S(1)} %bitcast.152, f32[4,512,1024]{2,1,0:T(8,128)} %fusion.172, f32[4,512,1024]{2,1,0:T(8,128)} %get-tuple-element.99, f32[4,512]{1,0:T(4,128)S(1)} %get-tuple-element.98), kind=kOutput, calls=%fused_computation.129 | convolution fusion | flops 283249664 | bytes 17571840 | tf_op jit(solution)/shard_map/hqk,khd->qhd/dot_general | solution.py:79
  382.6 2.1 add_convert_fusion
  386.5 47.9 %all-reduce.13.cloned.1.call-done = (bf16[512,256]{1,0:T(8,128)(2,1)}, bf16[512,256]{1,0:T(8,128)(2,1)}, bf16[256,512]{1,0:T(8,128)(2,1)}, bf16[512,1024]{1,0:T(8,128)(2,1)}, bf16[1024,512]{1,0:T(8,128)(2,1)}) async-done(((bf16[512,256]{1,0:T(8,128)(2,1)}, bf16[512,256]{1,0:T(8,128)(2,1)}, bf16[256,512]{1,0:T(8,128)(2,1)}, bf16[512,1024]{1,0:T(8,128)(2,1)}, bf16[1024,512]{1,0:T(8,128)(2,1)}), ...) | async-done | bytes 2883600 | tf_op jit(solution)/shard_map/psum | solution.py:244
  439.9 2.8 convert_multiply_fusion.2
  446.0 2.4 fusion.72
  448.4 4.5 multiply_add_fusion.1
  452.9 73.2 %all-gather.3.cloned.1.call-done = bf16[8192,256]{1,0:T(8,128)(2,1)} async-done(((bf16[512,256]{1,0:T(8,128)(2,1)}), bf16[8192,256]{1,0:T(8,128)(2,1)}) %all-gather.3.cloned.1.call-update) | async-done | bytes 4194320 | tf_op jit(solution)/shard_map/all_gather | solution.py:241
  526.1 2.9 reduce_sum.188
  (208 shorter events, 49.2 us)
Async XLA Ops:
  7.2 111.4 %copy-start = (bf16[512,1024]{1,0:T(8,128)(2,1)S(1)}, bf16[512,1024]{1,0:T(8,128)(2,1)}, u32[]{:S(2)}) copy-start(bf16[512,1024]{1,0:T(8,128)(2,1)} %param.28) | copy-start | bytes 3145732
  7.2 4.7 copy-start.2
  7.2 4.7 copy-start.50
  7.2 108.0 %all-reduce.9.cloned.1.call-start = ((), (), s32[]{:S(2)}) async-start(), calls=%async_computation.1 | async-start | bytes 4194304 | tf_op jit(solution)/shard_map/psum | solution.py:164
  14.3 9.9 %copy-start.39 = (s32[32768]{0:T(1024)S(1)}, s32[32768]{0:T(1024)}, u32[]{:S(2)}) copy-start(s32[32768]{0:T(1024)} %param.21) | copy-start | bytes 393220
  15.1 12.7 %copy-start.33 = (bf16[512,256]{1,0:T(8,128)(2,1)S(1)}, bf16[512,256]{1,0:T(8,128)(2,1)}, u32[]{:S(2)}) copy-start(bf16[512,256]{1,0:T(8,128)(2,1)} %param.23) | copy-start | bytes 786436
  15.9 6.5 %copy-start.11 = (bf16[2048,256]{0,1:T(8,128)(2,1)}, bf16[2048,256]{0,1:T(8,128)(2,1)S(1)}, u32[]{:S(2)}) copy-start(bf16[2048,256]{0,1:T(8,128)(2,1)S(1)} %convolution_convert_fusion.5) | copy-start | bytes 3145732
  16.8 16.4 %collective-permute-start = (bf16[256,512]{0,1:T(8,128)(2,1)}, bf16[256,512]{0,1:T(8,128)(2,1)}, u32[]{:S(2)}, u32[]{:S(2)}) collective-permute-start(bf16[256,512]{0,1:T(8,128)(2,1)} %get-tuple-element.74), channel_id=1, source_target_pairs={{0,2},{2,4},{4,6},{6,8},{8,10},{10,12},{12,14},{14,16},{16,18},{18... | collective-permute-start | bytes 786440 | tf_op jit(solution)/shard_map/ppermute | solution.py:21
  22.4 12.7 %collective-permute-start.1 = (bf16[256,512]{0,1:T(8,128)(2,1)}, bf16[256,512]{0,1:T(8,128)(2,1)}, u32[]{:S(2)}, u32[]{:S(2)}) collective-permute-start(bf16[256,512]{0,1:T(8,128)(2,1)} %get-tuple-element.75), channel_id=1, source_target_pairs={{2,0},{4,2},{6,4},{8,6},{10,8},{12,10},{14,12},{16,14},{18,16},{20... | collective-permute-start | bytes 786440 | tf_op jit(solution)/shard_map/ppermute | solution.py:23
  24.2 10.9 %copy-start.10 = (bf16[2048,256]{0,1:T(8,128)(2,1)S(1)}, bf16[2048,256]{0,1:T(8,128)(2,1)}, u32[]{:S(2)}) copy-start(bf16[2048,256]{0,1:T(8,128)(2,1)} %copy-done.9) | copy-start | bytes 3145732
  24.2 10.9 %copy-start.12 = (bf16[2048,256]{0,1:T(8,128)(2,1)S(1)}, bf16[2048,256]{0,1:T(8,128)(2,1)}, u32[]{:S(2)}) copy-start(bf16[2048,256]{0,1:T(8,128)(2,1)} %copy-done.11) | copy-start | bytes 3145732
  31.1 20.5 %copy-start.40 = (bf16[512,256]{0,1:T(8,128)(2,1)}, bf16[512,256]{0,1:T(8,128)(2,1)S(1)}, u32[]{:S(2)}) copy-start(bf16[512,256]{0,1:T(8,128)(2,1)S(1)} %get-tuple-element.87) | copy-start | bytes 786436
  59.0 5.8 %copy-start.42 = (bf16[512,256]{0,1:T(8,128)(2,1)S(1)}, bf16[512,256]{0,1:T(8,128)(2,1)}, u32[]{:S(2)}) copy-start(bf16[512,256]{0,1:T(8,128)(2,1)} %get-tuple-element.88) | copy-start | bytes 786436
  85.5 5.8 %copy-start.44 = (bf16[256,512]{1,0:T(8,128)(2,1)S(1)}, bf16[256,512]{1,0:T(8,128)(2,1)}, u32[]{:S(2)}) copy-start(bf16[256,512]{1,0:T(8,128)(2,1)} %param.26) | copy-start | bytes 786436
  85.5 5.8 %copy-start.54 = (bf16[4,64,512]{2,1,0:T(8,128)(2,1)S(1)}, bf16[4,64,512]{2,1,0:T(8,128)(2,1)}, u32[]{:S(2)}) copy-start(bf16[4,64,512]{2,1,0:T(8,128)(2,1)} %fusion.92) | copy-start | bytes 786436
  85.5 5.8 %copy-start.56 = (bf16[4,64,512]{2,1,0:T(8,128)(2,1)S(1)}, bf16[4,64,512]{2,1,0:T(8,128)(2,1)}, u32[]{:S(2)}) copy-start(bf16[4,64,512]{2,1,0:T(8,128)(2,1)} %fusion.101) | copy-start | bytes 786436
  85.6 5.8 %copy-start.58 = (bf16[4,64,512]{2,1,0:T(8,128)(2,1)S(1)}, bf16[4,64,512]{2,1,0:T(8,128)(2,1)}, u32[]{:S(2)}) copy-start(bf16[4,64,512]{2,1,0:T(8,128)(2,1)} %fusion.98) | copy-start | bytes 786436
  93.5 25.1 %copy-start.52 = (f32[512]{0:T(512)S(1)}, f32[512]{0:T(512)}, u32[]{:S(2)}) copy-start(f32[512]{0:T(512)} %param.27) | copy-start | bytes 6148
  93.5 61.6 %all-reduce.11.cloned.1.call-start = ((), (), s32[]{:S(2)}) async-start(), calls=%async_computation.2 | async-start | bytes 4194304 | tf_op jit(solution)/shard_map/psum | solution.py:177
  121.4 5.3 copy-start.62
  132.5 302.0 %all-reduce.13.cloned.1.call-start = ((), (), s32[]{:S(2)}) async-start(), calls=%async_computation.5 | async-start | bytes 5767168 | tf_op jit(solution)/shard_map/psum | solution.py:244
  132.5 6.5 %copy-start.21 = (bf16[2048,512]{1,0:T(8,128)(2,1)S(1)}, bf16[2048,512]{1,0:T(8,128)(2,1)}, u32[]{:S(2)}) copy-start(bf16[2048,512]{1,0:T(8,128)(2,1)} %param.20) | copy-start | bytes 6291460
  132.5 6.5 %copy-start.63 = (f32[2048,1024]{1,0:T(8,128)S(1)}, f32[2048,1024]{1,0:T(8,128)}, u32[]{:S(2)}) copy-start(f32[2048,1024]{1,0:T(8,128)} %copy-done.62) | copy-start | bytes 25165828
  155.1 7.4 %slice-start.6 = ((s8[8388608]{0:T(1024)(128)(4,1)}), s8[4194304]{0:T(1024)(128)(4,1)S(1)}, s32[]{:S(2)}) async-start(s8[8388608]{0:T(1024)(128)(4,1)} %bitcast.189), calls=%async_computation.13 | async-start | bytes 8388608
  161.6 8.5 %slice-start.4 = ((s8[8388608]{0:T(1024)(128)(4,1)}), s8[4194304]{0:T(1024)(128)(4,1)S(1)}, s32[]{:S(2)}) async-start(s8[8388608]{0:T(1024)(128)(4,1)} %bitcast.187), calls=%async_computation.11 | async-start | bytes 8388608
  162.5 7.6 %slice-start.5 = ((s8[8388608]{0:T(1024)(128)(4,1)}), s8[4194304]{0:T(1024)(128)(4,1)S(1)}, s32[]{:S(2)}) async-start(s8[8388608]{0:T(1024)(128)(4,1)} %bitcast.187), calls=%async_computation.12 | async-start | bytes 8388608
  165.5 11.0 %slice-start = ((s8[8388608]{0:T(1024)(128)(4,1)}), s8[4194304]{0:T(1024)(128)(4,1)S(1)}, s32[]{:S(2)}) async-start(s8[8388608]{0:T(1024)(128)(4,1)} %bitcast.183), calls=%async_computation.7 | async-start | bytes 8388608
  170.1 6.5 %slice-start.1 = ((s8[8388608]{0:T(1024)(128)(4,1)}), s8[4194304]{0:T(1024)(128)(4,1)S(1)}, s32[]{:S(2)}) async-start(s8[8388608]{0:T(1024)(128)(4,1)} %bitcast.183), calls=%async_computation.8 | async-start | bytes 8388608
  172.0 10.3 %slice-start.2 = ((s8[8388608]{0:T(1024)(128)(4,1)}), s8[4194304]{0:T(1024)(128)(4,1)S(1)}, s32[]{:S(2)}) async-start(s8[8388608]{0:T(1024)(128)(4,1)} %bitcast.185), calls=%async_computation.9 | async-start | bytes 8388608
  176.6 5.7 %slice-start.3 = ((s8[8388608]{0:T(1024)(128)(4,1)}), s8[4194304]{0:T(1024)(128)(4,1)S(1)}, s32[]{:S(2)}) async-start(s8[8388608]{0:T(1024)(128)(4,1)} %bitcast.185), calls=%async_computation.10 | async-start | bytes 8388608
  224.8 22.2 %copy-start.41 = (bf16[512,256]{0,1:T(8,128)(2,1)S(1)}, bf16[512,256]{0,1:T(8,128)(2,1)}, u32[]{:S(2)}) copy-start(bf16[512,256]{0,1:T(8,128)(2,1)} %copy-done.40) | copy-start | bytes 786436
  268.7 7.0 %copy-start.8 = (f32[2048,512]{1,0:T(8,128)S(1)}, f32[2048,512]{1,0:T(8,128)}, u32[]{:S(2)}) copy-start(f32[2048,512]{1,0:T(8,128)} %copy-done.7) | copy-start | bytes 12582916
  268.7 7.0 %copy-start.55 = (bf16[4,64,512]{2,1,0:T(8,128)(2,1)S(1)}, bf16[4,64,512]{2,1,0:T(8,128)(2,1)}, u32[]{:S(2)}) copy-start(bf16[4,64,512]{2,1,0:T(8,128)(2,1)} %fusion.92) | copy-start | bytes 786436
  268.7 7.0 %copy-start.57 = (bf16[4,64,512]{2,1,0:T(8,128)(2,1)S(1)}, bf16[4,64,512]{2,1,0:T(8,128)(2,1)}, u32[]{:S(2)}) copy-start(bf16[4,64,512]{2,1,0:T(8,128)(2,1)} %fusion.101) | copy-start | bytes 786436
  268.7 7.0 %copy-start.59 = (bf16[4,64,512]{2,1,0:T(8,128)(2,1)S(1)}, bf16[4,64,512]{2,1,0:T(8,128)(2,1)}, u32[]{:S(2)}) copy-start(bf16[4,64,512]{2,1,0:T(8,128)(2,1)} %fusion.98) | copy-start | bytes 786436
  268.7 7.0 %copy-start.61 = (bf16[4,64,512]{2,1,0:T(8,128)(2,1)S(1)}, bf16[4,64,512]{2,1,0:T(8,128)(2,1)}, u32[]{:S(2)}) copy-start(bf16[4,64,512]{2,1,0:T(8,128)(2,1)} %copy-done.60) | copy-start | bytes 786436
  269.7 11.2 %collective-permute-start.3 = (bf16[256,512]{0,1:T(8,128)(2,1)S(1)}, bf16[256,512]{0,1:T(8,128)(2,1)S(1)}, u32[]{:S(2)}, u32[]{:S(2)}) collective-permute-start(bf16[256,512]{0,1:T(8,128)(2,1)S(1)} %slice.275), channel_id=1, source_target_pairs={{2,0},{4,2},{6,4},{8,6},{10,8},{12,10},{14,12},{16,14},{18,16},{20... | collective-permute-start | bytes 786440 | tf_op jit(solution)/shard_map/ppermute | solution.py:23
  271.2 15.8 %collective-permute-start.2 = (bf16[256,512]{0,1:T(8,128)(2,1)S(1)}, bf16[256,512]{0,1:T(8,128)(2,1)S(1)}, u32[]{:S(2)}, u32[]{:S(2)}) collective-permute-start(bf16[256,512]{0,1:T(8,128)(2,1)S(1)} %slice.276), channel_id=1, source_target_pairs={{0,2},{2,4},{4,6},{6,8},{8,10},{10,12},{12,14},{14,16},{16,18},{18... | collective-permute-start | bytes 786440 | tf_op jit(solution)/shard_map/ppermute | solution.py:21
  291.6 21.8 %copy-start.37 = (bf16[1024,256]{0,1:T(8,128)(2,1)S(1)}, bf16[1024,256]{0,1:T(8,128)(2,1)}, u32[]{:S(2)}) copy-start(bf16[1024,256]{0,1:T(8,128)(2,1)} %get-tuple-element.82) | copy-start | bytes 1572868
  291.6 154.4 %reduce-scatter.2.cloned.1.call-start = ((), (), s32[]{:S(2)}) async-start(), calls=%async_computation.3 | async-start | bytes 3145728 | tf_op jit(solution)/shard_map/reduce_scatter | solution.py:231
  313.3 22.1 %copy-start.36 = (bf16[1024,256]{0,1:T(8,128)(2,1)S(1)}, bf16[1024,256]{0,1:T(8,128)(2,1)}, u32[]{:S(2)}) copy-start(bf16[1024,256]{0,1:T(8,128)(2,1)} %get-tuple-element.66) | copy-start | bytes 1572868
  335.5 22.1 %copy-start.35 = (bf16[1024,256]{0,1:T(8,128)(2,1)S(1)}, bf16[1024,256]{0,1:T(8,128)(2,1)}, u32[]{:S(2)}) copy-start(bf16[1024,256]{0,1:T(8,128)(2,1)} %get-tuple-element.72) | copy-start | bytes 1572868
  357.6 22.0 %copy-start.34 = (bf16[512,256]{1,0:T(8,128)(2,1)S(1)}, bf16[512,256]{1,0:T(8,128)(2,1)}, u32[]{:S(2)}) copy-start(bf16[512,256]{1,0:T(8,128)(2,1)} %param.23) | copy-start | bytes 786436
  384.7 141.4 %all-gather.3.cloned.1.call-start = ((), (), s32[]{:S(2)}) async-start(), calls=%async_computation.4 | async-start | bytes 4456448 | tf_op jit(solution)/shard_map/all_gather | solution.py:241
  434.4 8.3 %copy-start.23 = (bf16[1024,512]{1,0:T(8,128)(2,1)S(1)}, bf16[1024,512]{1,0:T(8,128)(2,1)}, u32[]{:S(2)}) copy-start(bf16[1024,512]{1,0:T(8,128)(2,1)} %get-tuple-element.63) | copy-start | bytes 3145732
  434.4 11.5 %copy-start.51 = (f32[512]{0:T(512)S(1)}, f32[512]{0:T(512)}, u32[]{:S(2)}) copy-start(f32[512]{0:T(512)} %param.22) | copy-start | bytes 6148
  439.9 8.5 %dynamic-slice-start = ((f32[2048]{0:T(1024)}, s32[]{:T(128)}), f32[1024]{0:T(1024)S(1)}, s32[]{:S(2)}) async-start(f32[2048]{0:T(1024)} %copy-done.49, s32[]{:T(128)} %select_n.30), calls=%async_computation.6 | async-start | bytes 8704 | tf_op jit(solution)/shard_map/dynamic-slice.31
  448.4 81.4 %copy-start.1 = (bf16[512,1024]{1,0:T(8,128)(2,1)S(1)}, bf16[512,1024]{1,0:T(8,128)(2,1)}, u32[]{:S(2)}) copy-start(bf16[512,1024]{1,0:T(8,128)(2,1)} %param.28) | copy-start | bytes 3145732
  (35 other events, 79.8 us)
Sparse Core Ops, SparseCore 0:
  93.6 21.5 all-reduce.8
  132.6 22.4 all-reduce.10
  291.7 142.6 all-reduce.12
  437.1 8.8 reduce-scatter.1
  449.2 76.8 all-gather.2
